TPU v7x, 32 devices: a whole 2x2x4 slice. The times are simulated.
32 devices in a mesh: row: 8 (over y, x, core), col: 4 (over z).
Axes of the slice: x: 2, y: 2, z: 4, core: 2. Of those that a mesh axis runs over, the one named last changes fastest.
Arguments:
- fixed_matrix_encodings: int32 [8192, 53248], P('row', 'col'), may hold values from 0 to 254, as said below
- line_restore_multiplier: float32 [8192], P('row'), may hold values from 0.001 to 0.01
- central_up_matrix: float32 [8192, 16], P('row', 'col'), may hold values from -1.5 to 1.5
- central_down_matrix: float32 [16, 53248], P('row', 'col'), may hold values from -1.5 to 1.5
- running_mean_up: float32 [8192, 16], P('row', 'col'), may hold values from -1.8 to 1.8
- squared_average_up: float32 [8192, 16], P('row', 'col'), may hold values from 0.05 to 0.5
- running_mean_down: float32 [16, 53248], P('row', 'col'), may hold values from -1.8 to 1.8
- squared_average_down: float32 [16, 53248], P('row', 'col'), may hold values from 0.05 to 0.5
- participant_change_up: bfloat16 [32, 8192, 16], P(('row', 'col')), may hold values from -48 to 48
- participant_change_down: bfloat16 [32, 16, 53248], P(('row', 'col')), may hold values from -48 to 48
- client_tallies: int32 [32, 2], P(('row', 'col')), may hold values from 1 to 64
Outputs:
- combined_normalized_entries: bfloat16 [8192, 53248], P('row', 'col')
- fresh_line_multipliers: float32 [8192], P('row')
- lora_b_next: float32 [8192, 16], P('row', 'col')
- lora_a_next: float32 [16, 53248], P('row', 'col')
- moment_b_next: float32 [8192, 16], P('row', 'col')
- second_b_next: float32 [8192, 16], P('row', 'col')
- moment_a_next: float32 [16, 53248], P('row', 'col')
- second_a_next: float32 [16, 53248], P('row', 'col')
Inputs may be any that keep to these rules, and one draw needn't show every extreme that they name: `fixed_matrix_encodings`: FP8 e4m3 bit patterns; the not-a-number patterns 127 and 255 never occur.
All inputs are finite; a program needn't handle non-finite values. Where the computation divides by a largest or mean magnitude, that divisor is 1e-20 or more.
Results may differ from a plain program's by a relative error of at most 0.0053.
Values may be sent and summed in bfloat16 or wider, within the bound.
A program may use at most 192 MiB of HBM per device.

v0:
```python
import jax
import jax.numpy as jnp
from jax import lax
from jax.sharding import PartitionSpec as P

first_decay = 0.9
second_decay = 0.99
server_rate = 0.1
adam_floor = 0.001
adapter_scale = 2.0
count_scale = 64.0
fp8_top = 448.0
peak_eps = 1e-06


def decode(codes):
    sign_bit = codes // 128
    exponent = codes // 8 % 16
    mantissa = codes % 8
    gaussian_sample = (8 + mantissa).astype(jnp.float32) * jnp.exp2(
        (exponent - 10).astype(jnp.float32)
    )
    subnormal = mantissa.astype(jnp.float32) * 2.0 ** (-9)
    magnitude = jnp.where(exponent > 0, gaussian_sample, subnormal)
    return magnitude * (1.0 - 2.0 * sign_bit.astype(jnp.float32))


def adaptive_update(param, moment, second, grad):
    moment_next = first_decay * moment + (1.0 - first_decay) * grad
    second_next = second_decay * second + (1.0 - second_decay) * grad * grad
    param_next = param - server_rate * moment_next / (jnp.sqrt(second_next) + adam_floor)
    return (param_next, moment_next, second_next)


def local(
    fixed_matrix_encodings,
    line_restore_multiplier,
    central_up_matrix,
    central_down_matrix,
    running_mean_up,
    squared_average_up,
    running_mean_down,
    squared_average_down,
    participant_change_up,
    participant_change_down,
    client_tallies,
):
    rows_count = lax.axis_size("row")
    cols_count = lax.axis_size("col")
    everyone = client_tallies.shape[0] * rows_count * cols_count
    weights = client_tallies.astype(jnp.float32) / (count_scale * everyone)
    summed_b = jnp.sum(
        weights[:, 0, None, None] * participant_change_up.astype(jnp.float32), axis=0
    )
    summed_a = jnp.sum(
        weights[:, 1, None, None] * participant_change_down.astype(jnp.float32), axis=0
    )
    depth_all, rank_all = summed_b.shape
    width_all = summed_a.shape[1]
    depth_dev = depth_all // rows_count
    rank_dev = rank_all // cols_count
    ranks_held = rank_all // rows_count
    width_dev = width_all // cols_count
    shaped_b = summed_b.reshape(rows_count, depth_dev, cols_count, rank_dev).transpose(0, 2, 1, 3)
    flat_b = shaped_b.reshape(rows_count * cols_count, depth_dev * rank_dev)
    shaped_a = summed_a.reshape(rows_count, ranks_held, cols_count, width_dev)
    shaped_a = shaped_a.transpose(0, 2, 1, 3).reshape(
        rows_count * cols_count, ranks_held, width_dev
    )
    gradient_b, gradient_a = (
        lax.psum_scatter(flat_b, ("row", "col"), scatter_dimension=0, tiled=True),
        lax.psum_scatter(shaped_a, ("row", "col"), scatter_dimension=0, tiled=True),
    )
    gradient_b = gradient_b.reshape(depth_dev, rank_dev)
    gradient_a = gradient_a[0]
    updated_factor_b, updated_moment_b, updated_variance_b = adaptive_update(
        central_up_matrix, running_mean_up, squared_average_up, gradient_b
    )
    updated_factor_a, updated_moment_a, updated_variance_a = adaptive_update(
        central_down_matrix, running_mean_down, squared_average_down, gradient_a
    )
    thin_up_matrix = lax.all_gather(
        updated_factor_b.astype(jnp.bfloat16), "col", axis=1, tiled=True
    )
    lowrank_a = lax.all_gather(updated_factor_a.astype(jnp.bfloat16), "row", axis=0, tiled=True)
    decode_weight = decode(fixed_matrix_encodings) * line_restore_multiplier[:, None]
    merged_weight = decode_weight + adapter_scale * jnp.dot(
        thin_up_matrix, lowrank_a, preferred_element_type=jnp.float32
    )
    local_peak = jnp.max(jnp.abs(merged_weight), axis=1)
    peak = lax.pmax(local_peak, "col") + peak_eps
    combined_normalized_entries = (merged_weight / peak[:, None]).astype(jnp.bfloat16)
    return (
        combined_normalized_entries,
        peak / fp8_top,
        updated_factor_b,
        updated_factor_a,
        updated_moment_b,
        updated_variance_b,
        updated_moment_a,
        updated_variance_a,
    )


def solution(mesh):
    return jax.shard_map(
        local,
        mesh=mesh,
        in_specs=(
            P("row", "col"),
            P("row"),
            P("row", "col"),
            P("row", "col"),
            P("row", "col"),
            P("row", "col"),
            P("row", "col"),
            P("row", "col"),
            P(("row", "col"), None, None),
            P(("row", "col"), None, None),
            P(("row", "col"), None),
        ),
        out_specs=(
            P("row", "col"),
            P("row"),
            P("row", "col"),
            P("row", "col"),
            P("row", "col"),
            P("row", "col"),
            P("row", "col"),
            P("row", "col"),
        ),
        check_vma=False,
    )
```

profile of v0, /device:TPU:0, one launch (start us, length us, event | category | flops | bytes accessed | tf_op | source)
XLA Modules:
  0.0 399.5 jit_solution(5018778585720609309)
XLA Ops:
  7.2 0.0 copy-start
  7.2 0.0 copy-start.2
  7.2 0.0 copy-start.1
  7.2 0.0 copy-start.3
  7.2 0.0 all-reduce.5.cloned.1.call-start
  7.3 0.7 convert_multiply_fusion.2
  7.9 0.6 fusion.16
  8.5 1.6 convert_multiply_fusion.1
  10.1 1.1 copy.57
  11.3 2.3 convert_multiply_fusion
  13.6 3.5 reshape.46
  17.1 6.3 %copy.56 = f32[8,2,4,13312]{3,1,2,0:T(2,128)} copy(f32[8,2,4,13312]{3,2,1,0:T(4,128)} %reshape.46) | data formatting | bytes 6815744 | tf_op jit(solution)/shard_map/reshape | solution.py:66
  23.4 9.6 %copy.52 = f32[8,1024,4,4]{3,1,2,0:T(8,128)} copy(f32[8,1024,4,4]{1,0,3,2:T(8,128)} %bitcast.32) | data formatting | bytes 1048576 | tf_op jit(solution)/shard_map/reshape | solution.py:64
  33.0 18.2 %reshape.44 = f32[32,4096]{1,0:T(8,128)} reshape(f32[8,4,1024,4]{3,2,1,0:T(8,128)} %bitcast.30) | data formatting | bytes 1048576 | tf_op jit(solution)/shard_map/reshape | solution.py:65
  51.2 0.0 all-reduce.5.cloned.1.call-update
  51.2 144.4 %all-reduce.5.cloned.1.call-done = (f32[32,4096]{1,0:T(8,128)}, f32[32,2,13312]{2,1,0:T(2,128)}) async-done(((f32[32,4096]{1,0:T(8,128)}, f32[32,2,13312]{2,1,0:T(2,128)}), (f32[32,4096]{1,0:T(8,128)}, f32[32,2,13312]{2,1,0:T(2,128)})) %all-reduce.5.cloned.1.call-update) | async-done | bytes 3932176
  195.6 1.0 dynamic-slice_reduce_fusion
  196.6 0.0 copy-done
  196.6 2.0 convert_bitcast_fusion
  198.6 9.7 %all-gather.1 = bf16[8,2,13312]{2,1,0:T(2,128)(2,1)S(1)} all-gather(bf16[1,2,13312]{2,1,0:T(2,128)(2,1)S(1)} %get-tuple-element.34), channel_id=1, replica_groups=mesh['row'=8,'col'=4] {'row'}, dimensions={0}, use_global_device_ids=true | all-gather | bytes 479232 | tf_op jit(solution)/shard_map/all_gather | solution.py:85
  208.3 0.2 reshape.51
  208.4 0.5 reshape.45
  209.0 0.2 copy.53
  209.2 0.0 copy-done.2
  209.2 0.0 copy-done.1
  209.2 1.4 convert_bitcast_fusion.1
  210.5 13.3 %all-gather = bf16[4,4,1024]{2,1,0:T(4,128)(2,1)S(1)} all-gather(bf16[1,4,1024]{2,1,0:T(4,128)(2,1)S(1)} %get-tuple-element.38), channel_id=1, replica_groups=mesh['row'=8,'col'=4] {'col'}, dimensions={0}, use_global_device_ids=true | all-gather | bytes 40960 | tf_op jit(solution)/shard_map/all_gather | solution.py:82
  223.9 0.0 copy-done.3
  223.9 130.8 %abs_reduce_fusion = (f32[1024]{0:T(1024)S(1)}, f32[1024,13312]{1,0:T(8,128)}) fusion(bf16[16,1024]{1,0:T(8,128)(2,1)S(1)} %reshape.49, bf16[16,13312]{1,0:T(8,128)(2,1)S(1)} %reshape.51, f32[1024]{0:T(1024)S(1)} %copy-done.3, s32[1024,13312]{1,0:T(8,128)} %param.11), kind=kOutput, calls=%fused_computation.20 | convolution fusion | flops 1240464384 | bytes 109518848 | tf_op jit(solution)/shard_map/dot_general | solution.py:87
  354.7 10.0 %pmax.7 = f32[1024]{0:T(1024)S(1)} all-reduce(f32[1024]{0:T(1024)S(1)} %get-tuple-element.46), channel_id=1, replica_groups=mesh['row'=8,'col'=4] {'col'}, use_global_device_ids=true, to_apply=%region_3.0 | all-reduce | flops 1024 | bytes 8192 | tf_op jit(solution)/shard_map/pmax | solution.py:91
  364.7 0.6 broadcast_multiply_fusion
  365.3 27.4 %divide_convert_fusion = bf16[1024,13312]{1,0:T(8,128)(2,1)} fusion(f32[1024,13312]{1,0:T(8,128)} %get-tuple-element.47, f32[1024]{0:T(1024)S(1)} %get-tuple-element.43), kind=kLoop, calls=%fused_computation.19 | loop fusion | flops 27262976 | bytes 81793024 | tf_op jit(solution)/shard_map/convert_element_type | solution.py:92
  (1 shorter events, 0.0 us)
Async XLA Ops:
  7.2 189.4 %copy-start = (f32[2,13312]{1,0:T(2,128)S(1)}, f32[2,13312]{1,0:T(2,128)}, u32[]{:S(2)}) copy-start(f32[2,13312]{1,0:T(2,128)} %param.14) | copy-start | bytes 319492
  7.2 202.0 %copy-start.2 = (f32[1024,4]{0,1:T(4,128)S(1)}, f32[1024,4]{0,1:T(4,128)}, u32[]{:S(2)}) copy-start(f32[1024,4]{0,1:T(4,128)} %param.15) | copy-start | bytes 49156
  7.2 202.0 %copy-start.1 = (f32[1024,4]{0,1:T(4,128)S(1)}, f32[1024,4]{0,1:T(4,128)}, u32[]{:S(2)}) copy-start(f32[1024,4]{0,1:T(4,128)} %param.13) | copy-start | bytes 49156
  7.2 216.7 %copy-start.3 = (f32[1024]{0:T(1024)S(1)}, f32[1024]{0:T(1024)}, u32[]{:S(2)}) copy-start(f32[1024]{0:T(1024)} %param.12) | copy-start | bytes 12292
  7.2 188.4 %all-reduce.5.cloned.1.call-start = ((), (), s32[]{:S(2)}) async-start(), calls=%async_computation | async-start | bytes 7864320
Sparse Core Ops, SparseCore 0:
  51.4 144.2 all-reduce.4
where the time goes:
time: 400 us
  waiting for transfers between devices  144 us (36%)
  matrix products  131 us (33%)
  local copies, waits for them, and re-layouts  41.2 us (10%)
  other arithmetic  36 us (9%)
  blocking collectives  33 us (8%)
  between operations  14.1 us (4%)
    unnamed x2, waiting for transfers between devices  144 us
    dot_general x1, matrix products, local(): jnp.dot(thin_up_matrix, lowrank_a, preferred_element_type=jnp.float32)  131 us
    convert_element_type x1, other arithmetic, local(): (merged_weight / peak[:, None]).astype(jnp.bfloat16)  27.4 us
    reshape x1, local copies, waits for them, and re-layouts, local(): flat_b = shaped_b.reshape(rows_count * cols_count, depth_dev * rank_dev)  18.2 us
    all_gather x1, blocking collectives, local(): lax.all_gather(updated_factor_b.astype(jnp.bfloat16), 'col', axis=1, tile...  13.3 us
    pmax x1, blocking collectives, local(): peak = lax.pmax(local_peak, 'col') + peak_eps  10 us
    reshape x2, local copies, waits for them, and re-layouts, local(): shaped_a = summed_a.reshape(rows_count, ranks_held, cols_count, width_dev)  9.85 us
    all_gather x1, blocking collectives, local(): lax.all_gather(updated_factor_a.astype(jnp.bfloat16), 'row', axis=0, tile...  9.68 us
  transfers between devices with their start and end apart: 1, of which 1 were waited for; matrix products, arithmetic and copies ran while one was open for 0% of the time, Pallas kernels for 0%

commit v1 on v0

v1 whole, which is shorter than its diff:
```python
import functools

import jax
import jax.numpy as jnp
from jax import lax
from jax.experimental import pallas as pl
from jax.experimental.pallas import tpu as pltpu
from jax.sharding import PartitionSpec as P

first_decay = 0.9
second_decay = 0.99
server_rate = 0.1
adam_floor = 0.001
adapter_scale = 2.0
count_scale = 64.0
fp8_top = 448.0
peak_eps = 1e-06
MESH = pl.DeviceIdType.MESH
LANES = 128
decode_lines = 32
merge_lines = 128
code_slots = 3


def tile_of(width, limit):
    best = LANES
    for tile in range(LANES, limit + 1, LANES):
        if width % tile == 0:
            best = tile
    return best


def adaptive_update(param, moment, second, grad):
    moment_next = first_decay * moment + (1.0 - first_decay) * grad
    second_next = second_decay * second + (1.0 - second_decay) * grad * grad
    param_next = param - server_rate * moment_next / (jnp.sqrt(second_next) + adam_floor)
    return (param_next, moment_next, second_next)


def scaled_decode(codes):
    low = codes & 127
    mantissa = codes & 7
    mantissa = jnp.where(low > 7, mantissa | 8, mantissa)
    magnitude = mantissa << jnp.maximum(low >> 3, 1)
    return jnp.where(codes > 127, -magnitude, magnitude).astype(jnp.float32)


def merge_kernel(
    rows_count, cols_count,
    codes, scale, pb, mb, vb, pa, ma, va, delta_b, delta_a, weight,
    merged, peak_wide, peak_out, nb, nmb, nvb, na, nma, nva,
    dense, code_buf, got_b, got_a, got_w, fac_b, fac_a, all_b, all_a, wide_b, wide_a,
    left, right, scale_wide, top, top_send, got_top,
    code_sem, out_sem, send_sem, recv_sem, gather_send, gather_recv, own_sem,
):
    my_row, my_col = lax.axis_index("row"), lax.axis_index("col")
    count = rows_count * cols_count
    me = my_row * cols_count + my_col
    depth, width = dense.shape
    steps = depth // decode_lines
    tile = tile_of(width, 1024)
    tiles = width // tile
    rank_b, rank_a = pb.shape[0], pa.shape[0]

    def fetch(i):
        slot = lax.rem(i, code_slots)
        return pltpu.make_async_copy(
            codes.at[pl.ds(i * decode_lines, decode_lines)], code_buf.at[slot], code_sem.at[slot]
        )

    for i in range(code_slots):
        fetch(i).start()

    barrier = pltpu.get_barrier_semaphore()

    def greet(k, _):
        to = lax.rem(me + k, count)
        pl.semaphore_signal(
            barrier, inc=1, device_id=(to // cols_count, lax.rem(to, cols_count)), device_id_type=MESH
        )
        return 0

    lax.fori_loop(1, count, greet, 0)
    pl.semaphore_wait(barrier, count - 1)

    def block_a(row, col):
        return delta_a.at[row, :, pl.ds(pl.multiple_of(col * width, LANES), width)]

    def block_b(row, col):
        return delta_b.at[col, :, pl.ds(pl.multiple_of(row * depth, LANES), depth)]

    def exchange(to, source):
        row, col = to // cols_count, lax.rem(to, cols_count)
        parts = (
            (weight, got_w.at[source]),
            (block_b(row, col), got_b.at[source]),
            (block_a(row, col), got_a.at[source]),
        )
        return [
            pltpu.make_async_remote_copy(
                src_ref=src, dst_ref=dst, send_sem=send_sem.at[n, to], recv_sem=recv_sem.at[n, source],
                device_id=(row, col), device_id_type=MESH,
            )
            for n, (src, dst) in enumerate(parts)
        ]

    def send(k, _):
        for copy in exchange(lax.rem(me + k, count), me):
            copy.start()
        return 0

    lax.fori_loop(1, count, send, 0)
    own = [
        pltpu.make_async_copy(weight, got_w.at[me], own_sem.at[0]),
        pltpu.make_async_copy(block_b(my_row, my_col), got_b.at[me], own_sem.at[1]),
        pltpu.make_async_copy(block_a(my_row, my_col), got_a.at[me], own_sem.at[2]),
    ]
    for copy in own:
        copy.start()

    for b in range(depth // LANES):
        line = jnp.broadcast_to(scale[b : b + 1, :] * 2.0 ** (-10), (LANES, LANES))
        scale_wide[b * LANES : (b + 1) * LANES, :] = line.T

    def decode_step(i, _):
        slot = lax.rem(i, code_slots)
        fetch(i).wait()

        def column(j, _):
            at = pl.ds(pl.multiple_of(j * tile, LANES), tile)
            for g in range(decode_lines // 16):
                value = scaled_decode(code_buf[slot, g * 16 : (g + 1) * 16, at])
                dense[pl.ds(pl.multiple_of(i * decode_lines + g * 16, 16), 16), at] = value.astype(
                    jnp.bfloat16
                )
            return 0

        lax.fori_loop(0, tiles, column, 0)

        @pl.when(i + code_slots < steps)
        def _():
            fetch(i + code_slots).start()

        return 0

    lax.fori_loop(0, steps, decode_step, 0)

    for copy in own:
        copy.wait()

    def arrive(k, _):
        source = lax.rem(me + k, count)
        for copy in exchange(source, source):
            copy.wait_recv()
        return 0

    lax.fori_loop(1, count, arrive, 0)

    def summed(got, which, at, shape):
        def add(s, total):
            return total + got_w[s, which : which + 1, 0:1] * got[s, :, at].astype(jnp.float32)

        return lax.fori_loop(0, count, add, jnp.zeros(shape, jnp.float32), unroll=8)

    grad_b = summed(got_b, 0, slice(None), (rank_b, depth))
    p, m, v = adaptive_update(pb[...], mb[...], vb[...], grad_b)
    nb[...] = p
    nmb[...] = m
    nvb[...] = v
    fac_b[...] = p.astype(jnp.bfloat16)

    def gather_b(to, source):
        return pltpu.make_async_remote_copy(
            src_ref=fac_b, dst_ref=all_b.at[source], send_sem=gather_send.at[0, to],
            recv_sem=gather_recv.at[0, source], device_id=(my_row, to), device_id_type=MESH,
        )

    def gather_a(to, source):
        return pltpu.make_async_remote_copy(
            src_ref=fac_a, dst_ref=all_a.at[source], send_sem=gather_send.at[1, to],
            recv_sem=gather_recv.at[1, source], device_id=(to, my_col), device_id_type=MESH,
        )

    for k in range(1, cols_count):
        gather_b(lax.rem(my_col + k, cols_count), my_col).start()
    own_b = pltpu.make_async_copy(fac_b, all_b.at[my_col], own_sem.at[0])
    own_b.start()

    def update_a(j, _):
        at = pl.ds(pl.multiple_of(j * tile, LANES), tile)
        grad = summed(got_a, 1, at, (rank_a, tile))
        p, m, v = adaptive_update(pa[:, at], ma[:, at], va[:, at], grad)
        na[:, at] = p
        nma[:, at] = m
        nva[:, at] = v
        fac_a[:, at] = p.astype(jnp.bfloat16)
        return 0

    lax.fori_loop(0, tiles, update_a, 0)
    for k in range(1, rows_count):
        gather_a(lax.rem(my_row + k, rows_count), my_row).start()
    own_a = pltpu.make_async_copy(fac_a, all_a.at[my_row], own_sem.at[1])
    own_a.start()

    own_b.wait()
    for k in range(1, cols_count):
        source = lax.rem(my_col + k, cols_count)
        gather_b(source, source).wait_recv()
    for c in range(cols_count):
        wide_b[c * rank_b : (c + 1) * rank_b, :] = all_b[c].astype(jnp.float32)
    left[...] = wide_b[...].T.astype(jnp.bfloat16)

    own_a.wait()
    for k in range(1, rows_count):
        source = lax.rem(my_row + k, rows_count)
        gather_a(source, source).wait_recv()

    def assemble(j, _):
        at = pl.ds(pl.multiple_of(j * tile, LANES), tile)
        for r in range(rows_count):
            wide_a[r * rank_a : (r + 1) * rank_a, :] = all_a[r, :, at].astype(jnp.float32)
        right[:, at] = wide_a[...].astype(jnp.bfloat16)
        return 0

    lax.fori_loop(0, tiles, assemble, 0)

    def put(i):
        lines = pl.ds(pl.multiple_of(i * merge_lines, merge_lines), merge_lines)
        return pltpu.make_async_copy(dense.at[lines], merged.at[lines], out_sem.at[i])

    def merge_step(i, _):
        lines = pl.ds(pl.multiple_of(i * merge_lines, merge_lines), merge_lines)
        top[lines, :] = jnp.zeros((merge_lines, LANES), jnp.float32)

        def column(j, _):
            at = pl.ds(pl.multiple_of(j * tile, LANES), tile)
            product = jnp.dot(left[lines, :], right[:, at], preferred_element_type=jnp.float32)
            for g in range(merge_lines // 16):
                group = pl.ds(pl.multiple_of(i * merge_lines + g * 16, 16), 16)
                line_scale = scale_wide[group, :]
                highest = top[group, :]
                for t in range(tile // LANES):
                    lane = pl.ds(pl.multiple_of(j * tile + t * LANES, LANES), LANES)
                    value = dense[group, lane].astype(jnp.float32) * line_scale
                    value = value + adapter_scale * product[
                        g * 16 : (g + 1) * 16, t * LANES : (t + 1) * LANES
                    ]
                    highest = jnp.maximum(highest, jnp.abs(value))
                    dense[group, lane] = value.astype(jnp.bfloat16)
                top[group, :] = highest
            return 0

        lax.fori_loop(0, tiles, column, 0)
        put(i).start()
        return 0

    lax.fori_loop(0, depth // merge_lines, merge_step, 0)

    for b in range(depth // LANES):
        square = top[b * LANES : (b + 1) * LANES, :]
        top_send[b : b + 1, :] = jnp.max(square.T, axis=0, keepdims=True)

    def gather_top(to, source):
        return pltpu.make_async_remote_copy(
            src_ref=top_send, dst_ref=got_top.at[source], send_sem=gather_send.at[2, to],
            recv_sem=gather_recv.at[2, source], device_id=(my_row, to), device_id_type=MESH,
        )

    for k in range(1, cols_count):
        gather_top(lax.rem(my_col + k, cols_count), my_col).start()
    peak = top_send[...]
    for k in range(1, cols_count):
        source = lax.rem(my_col + k, cols_count)
        gather_top(source, source).wait_recv()
        peak = jnp.maximum(peak, got_top[source])
    peak = peak + peak_eps
    peak_out[...] = peak / fp8_top
    for b in range(depth // LANES):
        peak_wide[b * LANES : (b + 1) * LANES, :] = jnp.broadcast_to(
            1.0 / peak[b : b + 1, :], (LANES, LANES)
        ).T

    def drain(i, _):
        put(i).wait()
        return 0

    lax.fori_loop(0, depth // merge_lines, drain, 0)

    def sent(k, _):
        for copy in exchange(lax.rem(me + k, count), me):
            copy.wait_send()
        return 0

    lax.fori_loop(1, count, sent, 0)
    for k in range(1, cols_count):
        to = lax.rem(my_col + k, cols_count)
        gather_b(to, my_col).wait_send()
        gather_top(to, my_col).wait_send()
    for k in range(1, rows_count):
        gather_a(lax.rem(my_row + k, rows_count), my_row).wait_send()


def normalize_kernel(merged, inverse, out):
    for t in range(merged.shape[1] // LANES):
        at = slice(t * LANES, (t + 1) * LANES)
        out[:, at] = (merged[:, at].astype(jnp.float32) * inverse[...]).astype(jnp.bfloat16)


def local(
    fixed_matrix_encodings,
    line_restore_multiplier,
    central_up_matrix,
    central_down_matrix,
    running_mean_up,
    squared_average_up,
    running_mean_down,
    squared_average_down,
    participant_change_up,
    participant_change_down,
    client_tallies,
):
    rows_count = lax.axis_size("row")
    cols_count = lax.axis_size("col")
    count = rows_count * cols_count
    depth, width = fixed_matrix_encodings.shape
    rank_b = central_up_matrix.shape[1]
    rank_a = central_down_matrix.shape[0]
    rank = participant_change_down.shape[1]
    blocks = depth // LANES
    everyone = client_tallies.shape[0] * count
    weights = client_tallies.astype(jnp.float32) / (count_scale * everyone)
    weight = jnp.broadcast_to(weights[0][:, None], (2, LANES))
    delta_b = participant_change_up[0].T.reshape(cols_count, rank_b, depth * rows_count)
    delta_a = participant_change_down[0].reshape(rows_count, rank_a, width * cols_count)
    anywhere = pl.BlockSpec(memory_space=pl.ANY)
    vmem = pl.BlockSpec(memory_space=pltpu.VMEM)
    f32, bf16 = jnp.float32, jnp.bfloat16
    shape = jax.ShapeDtypeStruct
    outs = pl.pallas_call(
        functools.partial(merge_kernel, rows_count, cols_count),
        out_shape=[
            shape((depth, width), bf16),
            shape((depth, LANES), f32),
            shape((blocks, LANES), f32),
        ]
        + [shape((rank_b, depth), f32)] * 3
        + [shape((rank_a, width), f32)] * 3,
        in_specs=[anywhere] + [vmem] * 7 + [anywhere] * 2 + [vmem],
        out_specs=[anywhere] + [vmem] * 8,
        scratch_shapes=[
            pltpu.VMEM((depth, width), bf16),
            pltpu.VMEM((code_slots, decode_lines, width), jnp.int32),
            pltpu.VMEM((count, rank_b, depth), bf16),
            pltpu.VMEM((count, rank_a, width), bf16),
            pltpu.VMEM((count, 2, LANES), f32),
            pltpu.VMEM((rank_b, depth), bf16),
            pltpu.VMEM((rank_a, width), bf16),
            pltpu.VMEM((cols_count, rank_b, depth), bf16),
            pltpu.VMEM((rows_count, rank_a, width), bf16),
            pltpu.VMEM((rank, depth), f32),
            pltpu.VMEM((rank, tile_of(width, 1024)), f32),
            pltpu.VMEM((depth, rank), bf16),
            pltpu.VMEM((rank, width), bf16),
            pltpu.VMEM((depth, LANES), f32),
            pltpu.VMEM((depth, LANES), f32),
            pltpu.VMEM((blocks, LANES), f32),
            pltpu.VMEM((cols_count, blocks, LANES), f32),
            pltpu.SemaphoreType.DMA((code_slots,)),
            pltpu.SemaphoreType.DMA((depth // merge_lines,)),
            pltpu.SemaphoreType.DMA((3, count)),
            pltpu.SemaphoreType.DMA((3, count)),
            pltpu.SemaphoreType.DMA((3, max(rows_count, cols_count))),
            pltpu.SemaphoreType.DMA((3, max(rows_count, cols_count))),
            pltpu.SemaphoreType.DMA((3,)),
        ],
        compiler_params=pltpu.CompilerParams(
            collective_id=0, has_side_effects=True, vmem_limit_bytes=62_000_000
        ),
    )(
        fixed_matrix_encodings,
        line_restore_multiplier.reshape(blocks, LANES),
        central_up_matrix.T,
        running_mean_up.T,
        squared_average_up.T,
        central_down_matrix,
        running_mean_down,
        squared_average_down,
        delta_b,
        delta_a,
        weight,
    )
    merged, inverse, fresh, nb, nmb, nvb, na, nma, nva = outs
    step = 64
    normalized = pl.pallas_call(
        normalize_kernel,
        grid=(depth // step,),
        out_shape=shape((depth, width), bf16),
        in_specs=[
            pl.BlockSpec((step, width), lambda i: (i, 0)),
            pl.BlockSpec((step, LANES), lambda i: (i, 0)),
        ],
        out_specs=pl.BlockSpec((step, width), lambda i: (i, 0)),
    )(merged, inverse)
    return (normalized, fresh.reshape(depth), nb.T, na, nmb.T, nvb.T, nma, nva)


def solution(mesh):
    grid = P("row", "col")
    clients = P(("row", "col"), None, None)
    return jax.shard_map(
        local,
        mesh=mesh,
        in_specs=(grid, P("row"), grid, grid, grid, grid, grid, grid, clients, clients, P(("row", "col"), None)),
        out_specs=(grid, P("row"), grid, grid, grid, grid, grid, grid),
        check_vma=False,
    )
```

time: 400 us -> 165 us (0.41)
  Pallas kernels: 0 us -> 154 us
  waiting for transfers between devices: 144 us -> 0 us
  matrix products: 131 us -> 0 us
  other arithmetic: 36 us -> 0.66 us
  blocking collectives: 33 us -> 0 us
  local copies, waits for them, and re-layouts: 41.2 us -> 9.9 us
  between operations: 14.1 us -> 0.71 us
    pallas_call x0 -> x2, Pallas kernels: none -> 154 us  [the longest x1 128 us: local(): pl.pallas_call(functools.partial(merge_kernel, rows_count, cols_count), o...]
    unnamed x2 -> x0, waiting for transfers between devices: 144 us -> none
    dot_general x1 -> x0, matrix products: 131 us -> none  [local(): jnp.dot(thin_up_matrix, lowrank_a, preferred_element_type=jnp.float32)]
    reshape x6 -> x1, local copies, waits for them, and re-layouts: 38.3 us -> 1.76 us  [local(): participant_change_up[0].T.reshape(cols_count, rank_b, depth * rows_count)]
    convert_element_type x1 -> x0, other arithmetic: 27.4 us -> none  [local(): (merged_weight / peak[:, None]).astype(jnp.bfloat16)]
    all_gather x2 -> x0, blocking collectives: 23 us -> none  [the longest x1 13.3 us: local(): lax.all_gather(updated_factor_b.astype(jnp.bfloat16), 'col', axis=1, tile...]
    pmax x1 -> x0, blocking collectives: 10 us -> none  [local(): peak = lax.pmax(local_peak, 'col') + peak_eps]
  transfers between devices with their start and end apart: 1 -> 0, of which waited for: 1 -> 0; matrix products, arithmetic and copies ran while one was open for 0% -> 0% of each run, Pallas kernels for 0% -> 0%
where the time goes in v1:
time: 165 us
  Pallas kernels  154 us (93%)
  local copies, waits for them, and re-layouts  9.9 us (6%)
    pallas_call x1, Pallas kernels, local(): pl.pallas_call(functools.partial(merge_kernel, rows_count, cols_count), o...  128 us
    pallas_call x1, Pallas kernels, local(): pl.pallas_call(normalize_kernel, grid=(depth // step,), out_shape=shape((...  25.4 us
    unnamed x21, local copies, waits for them, and re-layouts  4.37 us

profile of v1, /device:TPU:0, one launch (start us, length us, event | category | flops | bytes accessed | tf_op | source)
XLA Modules:
  0.0 165.0 jit_solution(17164265412927029878)
XLA Ops:
  0.6 0.7 multiply_bitcast_fusion
  1.3 0.6 broadcast_in_dim.8.weight
  1.9 1.8 %reshape.27.delta_b = bf16[4,4,8192]{2,1,0:T(4,128)(2,1)} reshape(bf16[16,8192]{1,0:T(8,128)(2,1)} %bitcast.13) | data formatting | bytes 524288 | tf_op jit(solution)/shard_map/reshape | solution.py:333
  3.7 3.1 %reshape_squeeze.3.delta_a = bf16[8,2,53248]{2,1,0:T(2,128)(2,1)} reshape(bf16[1,16,53248]{2,1,0:T(8,128)(2,1)} %param.20) | data formatting | bytes 3407872 | tf_op jit(solution)/shard_map/reshape;squeeze | solution.py:334
  6.8 128.3 %shard_map.170 = (bf16[1024,13312]{1,0:T(8,128)(2,1)}, f32[1024,128]{1,0:T(8,128)}, f32[8,128]{1,0:T(8,128)}, f32[4,1024]{1,0:T(4,128)}, f32[4,1024]{1,0:T(4,128...) custom-call(s32[1024,13312]{1,0:T(8,128)} %codes.1, f32[8,128]{1,0:T(8,128)} %bitcast.20, ...), custom_call_target="tpu_custom_call" | custom-call | tf_op jit(solution)/shard_map/pallas_call | solution.py:339
  135.1 0.0 copy-start.6
  135.1 0.0 copy-start.5
  135.1 0.0 copy-start.2
  135.1 0.0 copy-start.4
  135.1 0.0 copy-start.3
  135.2 0.0 copy-start.1
  135.2 0.0 copy-start
  135.2 25.4 %shard_map.171 = bf16[1024,13312]{1,0:T(8,128)(2,1)} custom-call(bf16[1024,13312]{1,0:T(8,128)(2,1)} %get-tuple-element.17.merged, f32[1024,128]{1,0:T(8,128)} %get-tuple-element.18.inverse), custom_call_target="tpu_custom_call" | custom-call | tf_op jit(solution)/shard_map/pallas_call | solution.py:394
  160.6 0.0 copy-done.6
  160.6 0.6 copy.26
  161.2 0.0 copy-done.5
  161.2 0.6 copy.27
  161.8 0.0 copy-done.2
  161.8 0.6 copy.28
  162.5 0.0 copy-done.4
  162.5 0.6 copy.29
  163.1 0.0 copy-done.3
  163.1 0.6 copy.30
  163.7 0.0 copy-done.1
  163.7 0.6 copy.31
  164.3 0.0 copy-done
  164.3 0.6 copy.32
Async XLA Ops:
  135.1 25.5 %copy-start.6 = (f32[8,128]{1,0:T(8,128)S(1)}, f32[8,128]{1,0:T(8,128)}, u32[]{:S(2)}) copy-start(f32[8,128]{1,0:T(8,128)} %get-tuple-element.19) | copy-start | bytes 12292
  135.1 26.1 %copy-start.5 = (f32[4,1024]{1,0:T(4,128)S(1)}, f32[4,1024]{1,0:T(4,128)}, u32[]{:S(2)}) copy-start(f32[4,1024]{1,0:T(4,128)} %get-tuple-element.20) | copy-start | bytes 49156
  135.1 26.7 %copy-start.2 = (f32[2,13312]{1,0:T(2,128)S(1)}, f32[2,13312]{1,0:T(2,128)}, u32[]{:S(2)}) copy-start(f32[2,13312]{1,0:T(2,128)} %get-tuple-element.37) | copy-start | bytes 319492
  135.1 27.3 %copy-start.4 = (f32[4,1024]{1,0:T(4,128)S(1)}, f32[4,1024]{1,0:T(4,128)}, u32[]{:S(2)}) copy-start(f32[4,1024]{1,0:T(4,128)} %get-tuple-element.22) | copy-start | bytes 49156
  135.1 27.9 %copy-start.3 = (f32[4,1024]{1,0:T(4,128)S(1)}, f32[4,1024]{1,0:T(4,128)}, u32[]{:S(2)}) copy-start(f32[4,1024]{1,0:T(4,128)} %get-tuple-element.23) | copy-start | bytes 49156
  135.2 28.5 %copy-start.1 = (f32[2,13312]{1,0:T(2,128)S(1)}, f32[2,13312]{1,0:T(2,128)}, u32[]{:S(2)}) copy-start(f32[2,13312]{1,0:T(2,128)} %get-tuple-element.40) | copy-start | bytes 319492
  135.2 29.2 %copy-start = (f32[2,13312]{1,0:T(2,128)S(1)}, f32[2,13312]{1,0:T(2,128)}, u32[]{:S(2)}) copy-start(f32[2,13312]{1,0:T(2,128)} %get-tuple-element.41) | copy-start | bytes 319492

commit v2 on v1

--- a/solution.py
+++ b/solution.py
@@ -20,6 +20,7 @@
 decode_lines = 32
 merge_lines = 128
 code_slots = 3
+stage_slots = 2
 
 
 def tile_of(width, limit):
@@ -50,7 +51,7 @@
     codes, scale, pb, mb, vb, pa, ma, va, delta_b, delta_a, weight,
     merged, peak_wide, peak_out, nb, nmb, nvb, na, nma, nva,
     dense, code_buf, got_b, got_a, got_w, fac_b, fac_a, all_b, all_a, wide_b, wide_a,
-    left, right, scale_wide, top, top_send, got_top,
+    left, right, stage, scale_wide, top, top_send, got_top,
     code_sem, out_sem, send_sem, recv_sem, gather_send, gather_recv, own_sem,
 ):
     my_row, my_col = lax.axis_index("row"), lax.axis_index("col")
@@ -225,36 +226,40 @@
     lax.fori_loop(0, tiles, assemble, 0)
 
     def put(i):
+        slot = lax.rem(i, stage_slots)
         lines = pl.ds(pl.multiple_of(i * merge_lines, merge_lines), merge_lines)
-        return pltpu.make_async_copy(dense.at[lines], merged.at[lines], out_sem.at[i])
+        return pltpu.make_async_copy(stage.at[slot], merged.at[lines], out_sem.at[slot])
+
+    merge_steps = depth // merge_lines
 
     def merge_step(i, _):
+        slot = lax.rem(i, stage_slots)
         lines = pl.ds(pl.multiple_of(i * merge_lines, merge_lines), merge_lines)
-        top[lines, :] = jnp.zeros((merge_lines, LANES), jnp.float32)
-
-        def column(j, _):
-            at = pl.ds(pl.multiple_of(j * tile, LANES), tile)
-            product = jnp.dot(left[lines, :], right[:, at], preferred_element_type=jnp.float32)
-            for g in range(merge_lines // 16):
-                group = pl.ds(pl.multiple_of(i * merge_lines + g * 16, 16), 16)
-                line_scale = scale_wide[group, :]
-                highest = top[group, :]
-                for t in range(tile // LANES):
-                    lane = pl.ds(pl.multiple_of(j * tile + t * LANES, LANES), LANES)
-                    value = dense[group, lane].astype(jnp.float32) * line_scale
-                    value = value + adapter_scale * product[
-                        g * 16 : (g + 1) * 16, t * LANES : (t + 1) * LANES
-                    ]
-                    highest = jnp.maximum(highest, jnp.abs(value))
-                    dense[group, lane] = value.astype(jnp.bfloat16)
-                top[group, :] = highest
-            return 0
-
-        lax.fori_loop(0, tiles, column, 0)
+
+        @pl.when(i >= stage_slots)
+        def _():
+            put(i - stage_slots).wait()
+
+        factor = left[lines, :]
+        line_scale = scale_wide[lines, :]
+
+        def column(j, highest):
+            for t in range(tile // LANES):
+                lane = pl.ds(pl.multiple_of(j * tile + t * LANES, LANES), LANES)
+                product = jnp.dot(factor, right[:, lane], preferred_element_type=jnp.float32)
+                value = dense[lines, lane].astype(jnp.float32) * line_scale
+                value = value + adapter_scale * product
+                highest = jnp.maximum(highest, jnp.abs(value))
+                stage[slot, :, lane] = value.astype(jnp.bfloat16)
+            return highest
+
+        top[lines, :] = lax.fori_loop(
+            0, tiles, column, jnp.zeros((merge_lines, LANES), jnp.float32)
+        )
         put(i).start()
         return 0
 
-    lax.fori_loop(0, depth // merge_lines, merge_step, 0)
+    lax.fori_loop(0, merge_steps, merge_step, 0)
 
     for b in range(depth // LANES):
         square = top[b * LANES : (b + 1) * LANES, :]
@@ -284,7 +289,7 @@
         put(i).wait()
         return 0
 
-    lax.fori_loop(0, depth // merge_lines, drain, 0)
+    lax.fori_loop(merge_steps - stage_slots, merge_steps, drain, 0)
 
     def sent(k, _):
         for copy in exchange(lax.rem(me + k, count), me):
@@ -361,12 +366,13 @@
             pltpu.VMEM((rank, tile_of(width, 1024)), f32),
             pltpu.VMEM((depth, rank), bf16),
             pltpu.VMEM((rank, width), bf16),
+            pltpu.VMEM((stage_slots, merge_lines, width), bf16),
             pltpu.VMEM((depth, LANES), f32),
             pltpu.VMEM((depth, LANES), f32),
             pltpu.VMEM((blocks, LANES), f32),
             pltpu.VMEM((cols_count, blocks, LANES), f32),
             pltpu.SemaphoreType.DMA((code_slots,)),
-            pltpu.SemaphoreType.DMA((depth // merge_lines,)),
+            pltpu.SemaphoreType.DMA((stage_slots,)),
             pltpu.SemaphoreType.DMA((3, count)),
             pltpu.SemaphoreType.DMA((3, count)),
             pltpu.SemaphoreType.DMA((3, max(rows_count, cols_count))),

time: 165 us -> 134 us (0.81)
  Pallas kernels: 154 us -> 122 us
    pallas_call x1, Pallas kernels: 128 us -> 96.4 us  [local(): pl.pallas_call(functools.partial(merge_kernel, rows_count, cols_count), o...]
where the time goes in v2:
time: 134 us; the launch traced here: 133 us
  Pallas kernels  122 us (91%)
  local copies, waits for them, and re-layouts  9.9 us (7%)
    pallas_call x1, Pallas kernels, local(): pl.pallas_call(functools.partial(merge_kernel, rows_count, cols_count), o...  96.4 us
    pallas_call x1, Pallas kernels, local(): pl.pallas_call(normalize_kernel, grid=(depth // step,), out_shape=shape((...  25.4 us
    unnamed x21, local copies, waits for them, and re-layouts  4.37 us
    another operation x1, local copies, waits for them, and re-layouts, local(): participant_change_down[0].reshape(rows_count, rank_a, width * cols_count)  3.14 us

profile of v2, /device:TPU:0, one launch (start us, length us, event | category | flops | bytes accessed | tf_op | source)
XLA Modules:
  0.0 133.1 jit_solution(17779879150215597517)
XLA Ops:
  0.6 0.7 multiply_bitcast_fusion
  1.3 0.6 broadcast_in_dim.8.weight
  1.9 1.8 %reshape.27.delta_b = bf16[4,4,8192]{2,1,0:T(4,128)(2,1)} reshape(bf16[16,8192]{1,0:T(8,128)(2,1)} %bitcast.13) | data formatting | bytes 524288 | tf_op jit(solution)/shard_map/reshape | solution.py:338
  3.7 3.1 %reshape_squeeze.3.delta_a = bf16[8,2,53248]{2,1,0:T(2,128)(2,1)} reshape(bf16[1,16,53248]{2,1,0:T(8,128)(2,1)} %param.20) | data formatting | bytes 3407872 | tf_op jit(solution)/shard_map/reshape;squeeze | solution.py:339
  6.8 96.4 %shard_map.170 = (bf16[1024,13312]{1,0:T(8,128)(2,1)}, f32[1024,128]{1,0:T(8,128)}, f32[8,128]{1,0:T(8,128)}, f32[4,1024]{1,0:T(4,128)}, f32[4,1024]{1,0:T(4,128...) custom-call(s32[1024,13312]{1,0:T(8,128)} %codes.1, f32[8,128]{1,0:T(8,128)} %bitcast.20, ...), custom_call_target="tpu_custom_call" | custom-call | tf_op jit(solution)/shard_map/pallas_call | solution.py:344
  103.2 0.0 copy-start.6
  103.2 0.0 copy-start.5
  103.2 0.0 copy-start.2
  103.3 0.0 copy-start.4
  103.3 0.0 copy-start.3
  103.3 0.0 copy-start.1
  103.3 0.0 copy-start
  103.3 25.4 %shard_map.171 = bf16[1024,13312]{1,0:T(8,128)(2,1)} custom-call(bf16[1024,13312]{1,0:T(8,128)(2,1)} %get-tuple-element.17.merged, f32[1024,128]{1,0:T(8,128)} %get-tuple-element.18.inverse), custom_call_target="tpu_custom_call" | custom-call | tf_op jit(solution)/shard_map/pallas_call | solution.py:400
  128.7 0.0 copy-done.6
  128.7 0.6 copy.26
  129.3 0.0 copy-done.5
  129.3 0.6 copy.27
  129.9 0.0 copy-done.2
  129.9 0.6 copy.28
  130.6 0.0 copy-done.4
  130.6 0.6 copy.29
  131.2 0.0 copy-done.3
  131.2 0.6 copy.30
  131.8 0.0 copy-done.1
  131.8 0.6 copy.31
  132.4 0.0 copy-done
  132.4 0.6 copy.32
Async XLA Ops:
  103.2 25.5 %copy-start.6 = (f32[8,128]{1,0:T(8,128)S(1)}, f32[8,128]{1,0:T(8,128)}, u32[]{:S(2)}) copy-start(f32[8,128]{1,0:T(8,128)} %get-tuple-element.19) | copy-start | bytes 12292
  103.2 26.1 %copy-start.5 = (f32[4,1024]{1,0:T(4,128)S(1)}, f32[4,1024]{1,0:T(4,128)}, u32[]{:S(2)}) copy-start(f32[4,1024]{1,0:T(4,128)} %get-tuple-element.20) | copy-start | bytes 49156
  103.2 26.7 %copy-start.2 = (f32[2,13312]{1,0:T(2,128)S(1)}, f32[2,13312]{1,0:T(2,128)}, u32[]{:S(2)}) copy-start(f32[2,13312]{1,0:T(2,128)} %get-tuple-element.37) | copy-start | bytes 319492
  103.3 27.3 %copy-start.4 = (f32[4,1024]{1,0:T(4,128)S(1)}, f32[4,1024]{1,0:T(4,128)}, u32[]{:S(2)}) copy-start(f32[4,1024]{1,0:T(4,128)} %get-tuple-element.22) | copy-start | bytes 49156
  103.3 27.9 %copy-start.3 = (f32[4,1024]{1,0:T(4,128)S(1)}, f32[4,1024]{1,0:T(4,128)}, u32[]{:S(2)}) copy-start(f32[4,1024]{1,0:T(4,128)} %get-tuple-element.23) | copy-start | bytes 49156
  103.3 28.5 %copy-start.1 = (f32[2,13312]{1,0:T(2,128)S(1)}, f32[2,13312]{1,0:T(2,128)}, u32[]{:S(2)}) copy-start(f32[2,13312]{1,0:T(2,128)} %get-tuple-element.40) | copy-start | bytes 319492
  103.3 29.2 %copy-start = (f32[2,13312]{1,0:T(2,128)S(1)}, f32[2,13312]{1,0:T(2,128)}, u32[]{:S(2)}) copy-start(f32[2,13312]{1,0:T(2,128)} %get-tuple-element.41) | copy-start | bytes 319492
